TPU v7x, 32 devices: a whole 2x2x4 slice. The times are simulated.
32 devices in a mesh: xy: 16 (over z, y, core), gz: 2 (over x).
Axes of the slice: x: 2, y: 2, z: 4, core: 2. Of those that a mesh axis runs over, the one named last changes fastest.
Arguments:
- hidden_features: bfloat16 [16, 16, 16, 512], P('gz', None, 'xy'), may hold values from -6 to 6
- scaling_factors_prenormal: float32 [512], replicated, may hold values from 0.1 to 1.9
- attention_input_matrices: bfloat16 [3, 512, 1536], P(None, 'xy'), may hold values from -1 to 1
- final_projection_matrices: bfloat16 [3, 512, 512], P(None, 'xy'), may hold values from -0.25 to 0.25
- score_scaling: float32 [3, 8], replicated, may hold values from 0 to 40
- filled_pillar_positions: int32 [16, 16], P('xy'), may hold values from 0 to 15, as said below
- filled_pillar_totals: int32 [16], P('xy'), may hold values from 4 to 16, as said below
Outputs:
- block_out: bfloat16 [16, 16, 16, 512], P('gz', None, 'xy')
Inputs may be any that keep to these rules, and one draw needn't show every extreme that they name: Row t of filled_pillar_positions is a permutation of 0 to 15; an entry c names the column x = c, y = t. `filled_pillar_totals`: some tile has all of its 16 columns occupied.
All inputs are finite; a program needn't handle non-finite values.
Results may differ from a plain program's by a relative error of at most 0.012.
Values may be sent and summed in bfloat16 or wider, within the bound.
No kernel may reach another device: no remote copies, remote signals or barrier semaphores. Data moves between devices by JAX's collectives and lax.ppermute only.
A program may use at most 64 MiB of HBM per device.

v0:
```python
import math

import jax
import jax.numpy as jnp
from jax import lax
from jax.sharding import PartitionSpec as P

EPSILON = 1e-06


def rms_scale(vector_rows):
    return vector_rows * lax.rsqrt(
        jnp.mean(vector_rows * vector_rows, axis=-1, keepdims=True) + EPSILON
    )


def project_qkv(tokens_in, w_project, attention_parts_number):
    projected = jnp.dot(tokens_in, w_project, preferred_element_type=jnp.float32)
    outer_shape = projected.shape[:-1]
    channels = w_project.shape[0]
    split_rows = projected.reshape(
        outer_shape + (3, attention_parts_number, channels // attention_parts_number)
    )
    queries = (
        rms_scale(split_rows[..., 0, :, :]).reshape(outer_shape + (channels,)).astype(jnp.bfloat16)
    )
    key_rows = (
        rms_scale(split_rows[..., 1, :, :]).reshape(outer_shape + (channels,)).astype(jnp.bfloat16)
    )
    values = split_rows[..., 2, :, :].reshape(outer_shape + (channels,)).astype(jnp.bfloat16)
    return (queries, key_rows, values)


def softmax_over_fibers(queries, key_rows, values, temper_row):
    attention_parts_number = temper_row.shape[0]
    outer_size, query_len, inner_size, channels = queries.shape
    key_len = key_rows.shape[1]
    head_dim = channels // attention_parts_number
    query_heads = queries.reshape(
        outer_size, query_len, inner_size, attention_parts_number, head_dim
    )
    key_heads = key_rows.reshape(outer_size, key_len, inner_size, attention_parts_number, head_dim)
    value_heads = values.reshape(outer_size, key_len, inner_size, attention_parts_number, head_dim)
    scores = jnp.einsum(
        "anbhd,ambhd->abhnm", query_heads, key_heads, preferred_element_type=jnp.float32
    )
    scores = scores * (temper_row / math.sqrt(head_dim))[None, None, :, None, None]
    weights = jax.nn.softmax(scores, axis=-1).astype(jnp.bfloat16)
    mixture = jnp.einsum(
        "abhnm,ambhd->anbhd", weights, value_heads, preferred_element_type=jnp.float32
    )
    return mixture.astype(jnp.bfloat16).reshape(outer_size, query_len, inner_size, channels)


def out_project(mixture, w_back):
    return jnp.dot(mixture, w_back, preferred_element_type=jnp.float32).astype(jnp.bfloat16)


def shards(
    hidden_features,
    scaling_factors_prenormal,
    attention_input_matrices,
    final_projection_matrices,
    score_scaling,
    filled_pillar_positions,
    filled_pillar_totals,
):
    full_qkv, full_out = (
        lax.all_gather(attention_input_matrices, "xy", axis=1, tiled=True),
        lax.all_gather(final_projection_matrices, "xy", axis=1, tiled=True),
    )
    attention_parts_number = score_scaling.shape[1]
    x_local, z_cells, y_rows, channels = hidden_features.shape
    normed = (rms_scale(hidden_features.astype(jnp.float32)) * scaling_factors_prenormal).astype(
        jnp.bfloat16
    )
    y_lines = normed.reshape(x_local * z_cells, y_rows, channels)
    local_query, local_keys, local_values = project_qkv(
        y_lines, full_qkv[1], attention_parts_number
    )
    query_along_y, keys_along_y, values_along_y = (
        lax.all_to_all(local_query, "xy", split_axis=0, concat_axis=1, tiled=True),
        lax.all_to_all(local_keys, "xy", split_axis=0, concat_axis=1, tiled=True),
        lax.all_to_all(local_values, "xy", split_axis=0, concat_axis=1, tiled=True),
    )
    y_mix = softmax_over_fibers(
        query_along_y[:, :, None, :],
        keys_along_y[:, :, None, :],
        values_along_y[:, :, None, :],
        score_scaling[1],
    )[:, :, 0, :]
    second_direction_answer = lax.all_to_all(
        out_project(y_mix, full_out[1]), "xy", split_axis=1, concat_axis=0, tiled=True
    ).reshape(hidden_features.shape)
    pieces = project_qkv(
        lax.all_to_all(normed, "gz", split_axis=1, concat_axis=0, tiled=True),
        full_qkv[0],
        attention_parts_number,
    )
    full_len, slab_part, items, _ = pieces[0].shape
    shaped = (1, full_len, slab_part * items, channels)
    x_mix = softmax_over_fibers(
        pieces[0].reshape(shaped),
        pieces[1].reshape(shaped),
        pieces[2].reshape(shaped),
        score_scaling[0],
    )
    result_rows = out_project(x_mix, full_out[0]).reshape(full_len, slab_part, items, channels)
    first_direction_answer = lax.all_to_all(
        result_rows, "gz", split_axis=0, concat_axis=1, tiled=True
    )
    cols_here = x_local * y_rows
    total_cols = filled_pillar_positions.shape[1]
    my_cols = lax.axis_index("gz") * cols_here + jnp.arange(cols_here, dtype=jnp.int32)
    live_rank = jnp.arange(total_cols, dtype=jnp.int32) < filled_pillar_totals[0]
    matches = filled_pillar_positions[0][None, :] == my_cols[:, None]
    live = jnp.any(jnp.logical_and(matches, live_rank[None, :]), axis=1)
    vertical_asking_terms, vertical_matching_terms, vertical_content_terms = project_qkv(
        normed, full_qkv[2], attention_parts_number
    )
    vertical_blended = softmax_over_fibers(
        vertical_asking_terms, vertical_matching_terms, vertical_content_terms, score_scaling[2]
    )
    z_full = out_project(vertical_blended, full_out[2])
    live_grid = live.reshape(x_local, 1, y_rows, 1)
    vertical_answer = jnp.where(live_grid, z_full, jnp.zeros_like(z_full))
    summed = (
        hidden_features.astype(jnp.float32)
        + first_direction_answer.astype(jnp.float32)
        + second_direction_answer.astype(jnp.float32)
    )
    summed = summed + vertical_answer.astype(jnp.float32)
    return summed.astype(jnp.bfloat16)


def solution(mesh):
    in_specs = (
        P("gz", None, "xy", None),
        P(),
        P(None, "xy", None),
        P(None, "xy", None),
        P(),
        P("xy", None),
        P("xy"),
    )
    out_specs = P("gz", None, "xy", None)
    return jax.shard_map(shards, mesh=mesh, in_specs=in_specs, out_specs=out_specs, check_vma=False)
```

profile of v0, /device:TPU:0, one launch (start us, length us, event | category | flops | bytes accessed | tf_op | source)
XLA Modules:
  0.0 148.3 jit_solution(13666185661406171766)
XLA Ops:
  6.5 0.7 all-gather.3.cloned.1.call-update
  7.3 1.0 fusion.23
  8.3 1.0 fusion.25
  9.3 0.7 copy.102
  10.0 4.2 %all-to-all-start = ((bf16[8,16,1,512]{3,0,2,1:T(8,128)(2,1)}), bf16[8,16,1,512]{3,0,2,1:T(8,128)(2,1)S(1)}, u32[]{:S(2)}, u32[]{:S(2)}) async-start(bf16[8,16,1,512]{3,0,2,1:T(8,128)(2,1)} %copy.102), calls=%async_computation | async-start | bytes 262144 | tf_op jit(solution)/shard_map/all_to_all | solution.py:96
  14.3 0.7 all-gather.5.cloned.1.call-update
  15.0 0.8 multiply_bitcast_fusion.2
  16.5 0.8 and_reduce_fusion
  17.3 1.5 %all-to-all-done = bf16[8,16,1,512]{3,0,2,1:T(8,128)(2,1)S(1)} async-done(((bf16[8,16,1,512]{3,0,2,1:T(8,128)(2,1)}), bf16[8,16,1,512]{3,0,2,1:T(8,128)(2,1)S(1)}, u32[]{:S(2)}, u32[]{:S(2)}) %all-to-all-start) | async-done | bytes 131104 | tf_op jit(solution)/shard_map/all_to_all | solution.py:96
  18.8 0.7 copy.103
  19.5 46.0 %all-gather.3.cloned.1.call-done = bf16[3,512,1536]{2,1,0:T(8,128)(2,1)} async-done(((bf16[3,32,1536]{2,1,0:T(8,128)(2,1)}), bf16[3,512,1536]{2,1,0:T(8,128)(2,1)}) %all-gather.3.cloned.1.call-update) | async-done | bytes 4718608 | tf_op jit(solution)/shard_map/all_gather | solution.py:69
  65.5 4.4 %slice_bitcast_fusion.2 = (bf16[1536,512]{0,1:T(8,128)(2,1)}, bf16[1536,512]{0,1:T(8,128)(2,1)S(1)}, bf16[1536,512]{0,1:T(8,128)(2,1)}) fusion(bf16[3,512,1536]{2,1,0:T(8,128)(2,1)} %all-gather.3.cloned.1.call-done), kind=kLoop, calls=%fused_computation.5 | loop fusion | bytes 9437184 | tf_op jit(solution)/shard_map/dot_general | solution.py:18
  69.9 1.7 %copy.104 = bf16[1536,512]{1,0:T(8,128)(2,1)S(1)} copy(bf16[1536,512]{0,1:T(8,128)(2,1)} %get-tuple-element.11) | data formatting | bytes 3145728 | tf_op jit(solution)/shard_map/dot_general | solution.py:18
  71.6 2.6 %copy.112 = bf16[1536,512]{1,0:T(8,128)(2,1)} copy(bf16[1536,512]{0,1:T(8,128)(2,1)} %get-tuple-element.13) | data formatting | bytes 3145728 | tf_op jit(solution)/shard_map/dot_general | solution.py:18
  74.3 2.0 %convolution_bitcast_fusion.2 = f32[128,1,3,8,64]{0,4,3,2,1:T(8,128)S(1)} fusion(bf16[128,512,1,1]{1,0,3,2:T(8,128)(2,1)S(1)} %bitcast.200, bf16[3,8,64,512]{3,2,1,0:T(8,128)(2,1)} %bitcast.199), kind=kOutput, calls=%fused_computation.8 | convolution fusion | flops 201326592 | bytes 2490368 | tf_op jit(solution)/shard_map/dot_general | solution.py:18
  76.3 0.9 copy-done
  77.3 0.5 broadcast.203
  77.8 1.2 reduce.26
  79.0 1.0 copy.180
  80.1 0.7 reshape.552
  80.8 3.5 %all-to-all-start.3 = ((bf16[16,2,2048]{2,1,0:T(2,128)(2,1)}), bf16[16,2,2048]{2,1,0:T(2,128)(2,1)S(1)}, u32[]{:S(2)}, u32[]{:S(2)}) async-start(bf16[16,2,2048]{2,1,0:T(2,128)(2,1)} %reshape.552), calls=%async_computation.3 | async-start | bytes 262144 | tf_op jit(solution)/shard_map/all_to_all | solution.py:82
  84.3 1.8 %convolution_bitcast_fusion.1 = f32[16,8,1,3,8,64]{5,1,4,3,0,2:T(8,128)S(1)} fusion(bf16[16,8,512,1,1]{2,1,4,3,0:T(8,128)(2,1)} %bitcast.207, bf16[3,8,64,512,1]{3,2,1,0,4:T(8,128)(2,1)S(1)} %bitcast.197), kind=kOutput, calls=%fused_computation.7 | convolution fusion | flops 201326592 | bytes 2490368 | tf_op jit(solution)/shard_map/dot_general | solution.py:18
  86.5 0.4 fusion.22
  86.9 0.8 fusion.60
  87.7 1.0 fusion.9
  88.7 0.6 reduce.25
  89.4 0.7 reshape.550
  90.1 0.7 copy.125
  90.8 0.9 convolution_bitcast_fusion
  91.8 0.4 all-to-all-done.3
  92.2 5.8 %all-to-all-start.4 = ((bf16[16,2,2048]{2,1,0:T(2,128)(2,1)}), bf16[16,2,2048]{2,1,0:T(2,128)(2,1)S(1)}, u32[]{:S(2)}, u32[]{:S(2)}) async-start(bf16[16,2,2048]{2,1,0:T(2,128)(2,1)} %reshape.550), calls=%async_computation.4 | async-start | bytes 262144 | tf_op jit(solution)/shard_map/all_to_all | solution.py:83
  98.3 1.0 slice.122
  99.6 0.6 reduce.27
  100.3 0.7 reshape.554
  101.0 5.2 %all-to-all-done.4 = bf16[16,2,2048]{2,1,0:T(2,128)(2,1)S(1)} async-done(((bf16[16,2,2048]{2,1,0:T(2,128)(2,1)}), bf16[16,2,2048]{2,1,0:T(2,128)(2,1)S(1)}, u32[]{:S(2)}, u32[]{:S(2)}) %all-to-all-start.4) | async-done | bytes 131104 | tf_op jit(solution)/shard_map/all_to_all | solution.py:83
  106.2 3.5 %all-to-all-start.2 = ((bf16[16,2,2048]{2,1,0:T(2,128)(2,1)}), bf16[16,2,2048]{2,1,0:T(2,128)(2,1)S(1)}, u32[]{:S(2)}, u32[]{:S(2)}) async-start(bf16[16,2,2048]{2,1,0:T(2,128)(2,1)} %reshape.554), calls=%async_computation.2 | async-start | bytes 262144 | tf_op jit(solution)/shard_map/all_to_all | solution.py:84
  109.8 2.0 %fusion.54 = (f32[8,8,16]{2,1,0:T(8,128)}, f32[8,8,16,16]{2,3,1,0:T(8,128)}) fusion(f32[8,16,1,3,8,64]{5,1,4,3,0,2:T(8,128)S(1)} %convolution_bitcast_fusion, f32[8]{0:T(128)S(1)} %get-tuple-element.19, f32[8,16,8]{1,2,0:T(8,128)S(1)} %get-tuple-element.27, f32[8,16,8]{1,2,0:T(8,128)S(1)} %get-tuple-element.28), kind=kOutput, calls=%fused_computation.99 | convolution fusion | flops 2408463 | bytes 1184256 | tf_op jit(solution)/shard_map/sub | solution.py:48
  112.4 5.2 %all-to-all-done.2 = bf16[16,2,2048]{2,1,0:T(2,128)(2,1)S(1)} async-done(((bf16[16,2,2048]{2,1,0:T(2,128)(2,1)}), bf16[16,2,2048]{2,1,0:T(2,128)(2,1)S(1)}, u32[]{:S(2)}, u32[]{:S(2)}) %all-to-all-start.2) | async-done | bytes 131104 | tf_op jit(solution)/shard_map/all_to_all | solution.py:84
  118.0 0.5 fusion.55
  119.1 1.3 convolution_convert_fusion.4
  120.4 0.7 copy.124
  121.2 3.6 %all-to-all-start.5 = ((bf16[8,16,512]{2,0,1:T(8,128)(2,1)}), bf16[8,16,512]{2,0,1:T(8,128)(2,1)S(1)}, u32[]{:S(2)}, u32[]{:S(2)}) async-start(bf16[8,16,512]{2,0,1:T(8,128)(2,1)} %copy.124), calls=%async_computation.5 | async-start | bytes 262144 | tf_op jit(solution)/shard_map/all_to_all | solution.py:92
  124.8 1.3 fusion.11
  126.4 0.9 fusion.12
  127.3 5.3 %all-to-all-done.5 = bf16[8,16,512]{2,0,1:T(8,128)(2,1)S(1)} async-done(((bf16[8,16,512]{2,0,1:T(8,128)(2,1)}), bf16[8,16,512]{2,0,1:T(8,128)(2,1)S(1)}, u32[]{:S(2)}, u32[]{:S(2)}) %all-to-all-start.5) | async-done | bytes 131104 | tf_op jit(solution)/shard_map/all_to_all | solution.py:92
  132.7 3.4 %all-to-all-start.1 = ((bf16[16,8,1,512]{3,1,2,0:T(8,128)(2,1)}), bf16[16,8,1,512]{3,1,2,0:T(8,128)(2,1)S(1)}, u32[]{:S(2)}, u32[]{:S(2)}) async-start(bf16[16,8,1,512]{3,1,2,0:T(8,128)(2,1)} %fusion.12), calls=%async_computation.1 | async-start | bytes 262144 | tf_op jit(solution)/shard_map/all_to_all | solution.py:109
  136.1 4.4 %all-to-all-done.1 = bf16[16,8,1,512]{3,1,2,0:T(8,128)(2,1)S(1)} async-done(((bf16[16,8,1,512]{3,1,2,0:T(8,128)(2,1)}), bf16[16,8,1,512]{3,1,2,0:T(8,128)(2,1)S(1)}, u32[]{:S(2)}, u32[]{:S(2)}) %all-to-all-start.1) | async-done | bytes 131104 | tf_op jit(solution)/shard_map/all_to_all | solution.py:109
  140.5 0.9 fusion.18
  (45 shorter events, 3.4 us)
Async XLA Ops:
  6.5 59.0 %all-gather.3.cloned.1.call-start = ((), (), s32[]{:S(2)}) async-start(), calls=%async_computation.6 | async-start | bytes 5013504 | tf_op jit(solution)/shard_map/all_gather | solution.py:69
  10.0 8.8 %all-to-all-start = ((bf16[8,16,1,512]{3,0,2,1:T(8,128)(2,1)}), bf16[8,16,1,512]{3,0,2,1:T(8,128)(2,1)S(1)}, u32[]{:S(2)}, u32[]{:S(2)}) async-start(bf16[8,16,1,512]{3,0,2,1:T(8,128)(2,1)} %copy.102), calls=%async_computation | async-start | bytes 262144 | tf_op jit(solution)/shard_map/all_to_all | solution.py:96
  14.3 104.9 %all-gather.5.cloned.1.call-start = ((), (), s32[]{:S(2)}) async-start(), calls=%async_computation.7 | async-start | bytes 1671168 | tf_op jit(solution)/shard_map/all_gather | solution.py:70
  76.2 0.9 copy-start
  80.8 11.4 %all-to-all-start.3 = ((bf16[16,2,2048]{2,1,0:T(2,128)(2,1)}), bf16[16,2,2048]{2,1,0:T(2,128)(2,1)S(1)}, u32[]{:S(2)}, u32[]{:S(2)}) async-start(bf16[16,2,2048]{2,1,0:T(2,128)(2,1)} %reshape.552), calls=%async_computation.3 | async-start | bytes 262144 | tf_op jit(solution)/shard_map/all_to_all | solution.py:82
  91.7 7.5 %copy-start.3 = (bf16[1,16,8,8,64]{4,1,3,2,0:T(8,128)(2,1)S(1)}, bf16[1,16,8,8,64]{4,1,3,2,0:T(8,128)(2,1)}, u32[]{:S(2)}) copy-start(bf16[1,16,8,8,64]{4,1,3,2,0:T(8,128)(2,1)} %fusion.9) | copy-start | bytes 393220
  92.2 14.1 %all-to-all-start.4 = ((bf16[16,2,2048]{2,1,0:T(2,128)(2,1)}), bf16[16,2,2048]{2,1,0:T(2,128)(2,1)S(1)}, u32[]{:S(2)}, u32[]{:S(2)}) async-start(bf16[16,2,2048]{2,1,0:T(2,128)(2,1)} %reshape.550), calls=%async_computation.4 | async-start | bytes 262144 | tf_op jit(solution)/shard_map/all_to_all | solution.py:83
  106.2 11.4 %all-to-all-start.2 = ((bf16[16,2,2048]{2,1,0:T(2,128)(2,1)}), bf16[16,2,2048]{2,1,0:T(2,128)(2,1)S(1)}, u32[]{:S(2)}, u32[]{:S(2)}) async-start(bf16[16,2,2048]{2,1,0:T(2,128)(2,1)} %reshape.554), calls=%async_computation.2 | async-start | bytes 262144 | tf_op jit(solution)/shard_map/all_to_all | solution.py:84
  118.8 6.0 %copy-start.4 = (f32[8,8,16]{2,1,0:T(8,128)S(1)}, f32[8,8,16]{2,1,0:T(8,128)}, u32[]{:S(2)}) copy-start(f32[8,8,16]{2,1,0:T(8,128)} %get-tuple-element.21) | copy-start | bytes 12292
  121.1 5.3 %copy-start.2 = (bf16[3,512,512]{2,1,0:T(8,128)(2,1)S(1)}, bf16[3,512,512]{2,1,0:T(8,128)(2,1)}, u32[]{:S(2)}) copy-start(bf16[3,512,512]{2,1,0:T(8,128)(2,1)} %all-gather.5.cloned.1.call-done) | copy-start | bytes 4718596
  121.2 11.5 %all-to-all-start.5 = ((bf16[8,16,512]{2,0,1:T(8,128)(2,1)}), bf16[8,16,512]{2,0,1:T(8,128)(2,1)S(1)}, u32[]{:S(2)}, u32[]{:S(2)}) async-start(bf16[8,16,512]{2,0,1:T(8,128)(2,1)} %copy.124), calls=%async_computation.5 | async-start | bytes 262144 | tf_op jit(solution)/shard_map/all_to_all | solution.py:92
  126.1 14.4 %copy-start.1 = (bf16[8,16,1,512]{3,1,2,0:T(8,128)(2,1)S(1)}, bf16[8,16,1,512]{3,1,2,0:T(8,128)(2,1)}, u32[]{:S(2)}) copy-start(bf16[8,16,1,512]{3,1,2,0:T(8,128)(2,1)} %param.7) | copy-start | bytes 393220
  132.7 7.8 %all-to-all-start.1 = ((bf16[16,8,1,512]{3,1,2,0:T(8,128)(2,1)}), bf16[16,8,1,512]{3,1,2,0:T(8,128)(2,1)S(1)}, u32[]{:S(2)}, u32[]{:S(2)}) async-start(bf16[16,8,1,512]{3,1,2,0:T(8,128)(2,1)} %fusion.12), calls=%async_computation.1 | async-start | bytes 262144 | tf_op jit(solution)/shard_map/all_to_all | solution.py:109
Sparse Core Ops, SparseCore 0:
  9.6 55.8 all-gather.2
  67.7 39.1 all-gather.4
where the time goes:
time: 149 us; the launch traced here: 148 us
  waiting for transfers between devices  69.6 us (47%)
  starting transfers between devices  24.1 us (16%)
  local copies, waits for them, and re-layouts  19.2 us (13%)
  between operations  14.4 us (10%)
  matrix products  13.7 us (9%)
  other arithmetic  7.31 us (5%)
    all_gather x1, waiting for transfers between devices, shards(): lax.all_gather(attention_input_matrices, 'xy', axis=1, tiled=True)  46 us
    dot_general x4, local copies, waits for them, and re-layouts, project_qkv(): jnp.dot(tokens_in, w_project, preferred_element_type=jnp.float32)  9.41 us
    all_to_all x1, starting transfers between devices, shards(): lax.all_to_all(local_keys, 'xy', split_axis=0, concat_axis=1, tiled=True)  5.78 us
    all_to_all x1, waiting for transfers between devices, shards(): lax.all_to_all(out_project(y_mix, full_out[1]), 'xy', split_axis=1, conca...  5.35 us
    all_to_all x1, waiting for transfers between devices, shards(): lax.all_to_all(local_keys, 'xy', split_axis=0, concat_axis=1, tiled=True)  5.24 us
    all_to_all x1, waiting for transfers between devices, shards(): lax.all_to_all(local_values, 'xy', split_axis=0, concat_axis=1, tiled=True)  5.21 us
    dot_general x3, matrix products, project_qkv(): jnp.dot(tokens_in, w_project, preferred_element_type=jnp.float32)  4.68 us
    unnamed x22, local copies, waits for them, and re-layouts  4.68 us
  transfers between devices with their start and end apart: 8, of which 7 were waited for; matrix products, arithmetic and copies ran while one was open for 25% of the time, Pallas kernels for 0%

commit v1 on v0

--- a/solution.py
+++ b/solution.py
@@ -1,8 +1,11 @@
+import functools
 import math
 
 import jax
 import jax.numpy as jnp
 from jax import lax
+from jax.experimental import pallas as pl
+from jax.experimental.pallas import tpu as pltpu
 from jax.sharding import PartitionSpec as P
 
 EPSILON = 1e-06
@@ -56,7 +59,7 @@
     return jnp.dot(mixture, w_back, preferred_element_type=jnp.float32).astype(jnp.bfloat16)
 
 
-def shards(
+def generic_shards(
     hidden_features,
     scaling_factors_prenormal,
     attention_input_matrices,
@@ -133,6 +136,332 @@
     return summed.astype(jnp.bfloat16)
 
 
+LANES = 128
+CORES = 2
+MASKED = -1e30
+BRANCH_CHUNKS = ((1,), (0, 2))
+
+
+def xy_swap(array, bit, count):
+    return lax.ppermute(array, "xy", [(i, i ^ bit) for i in range(count)])
+
+
+def gz_swap(array):
+    return lax.ppermute(array, "gz", [(0, 1), (1, 0)])
+
+
+def normed_rows(rows, gain):
+    wide = rows.astype(jnp.float32)
+    return (rms_scale(wide) * gain).astype(jnp.bfloat16)
+
+
+def my_group():
+    core = lax.rem(lax.axis_index("xy"), CORES)
+    return CORES * lax.axis_index("gz") + core
+
+
+def slice_weights_kernel(w_ref, *out_refs):
+    channels = w_ref.shape[2] // 3
+    core = lax.rem(lax.axis_index("xy"), CORES)
+    base = CORES * lax.axis_index("gz")
+    for chunk, branches in enumerate(BRANCH_CHUNKS):
+        for side, group in enumerate((base + core, base + 1 - core)):
+            out_ref = out_refs[2 * chunk + side]
+            for n, branch in enumerate(branches):
+                for part in range(3):
+                    start = pl.multiple_of(part * channels + group * LANES, LANES)
+                    out_ref[3 * n + part] = w_ref[branch, :, pl.ds(start, LANES)]
+
+
+def slice_weights(w_local):
+    rows = w_local.shape[1]
+    outs = []
+    for branches in BRANCH_CHUNKS:
+        outs += [jax.ShapeDtypeStruct((3 * len(branches), rows, LANES), w_local.dtype)] * 2
+    return pl.pallas_call(slice_weights_kernel, out_shape=outs, name="slice_weights")(w_local)
+
+
+def place_weights(piece_refs, w_ref, branch_count):
+    me = lax.axis_index("xy")
+    rows = piece_refs[0].shape[2]
+    for offset, piece_ref in enumerate(piece_refs):
+        for sub in range(CORES):
+            source = lax.bitwise_xor(me, CORES * offset + sub)
+            at = pl.ds(pl.multiple_of(source * rows, rows), rows)
+            for n in range(branch_count):
+                for part in range(3):
+                    w_ref[n, at, part * LANES : (part + 1) * LANES] = piece_ref[sub, 3 * n + part]
+
+
+def attend(tokens, w, scales, same_line, head_dim):
+    lane = lax.broadcasted_iota(jnp.int32, (1, LANES), 1)
+    first = lane < head_dim
+    head_a = lax.broadcasted_iota(jnp.int32, (LANES, LANES), 0) // head_dim
+    head_b = lax.broadcasted_iota(jnp.int32, (LANES, LANES), 1) // head_dim
+    same_head = (head_a == head_b).astype(jnp.float32).astype(jnp.bfloat16)
+
+    def head_norm(part):
+        squares = part * part
+        high = squares.astype(jnp.bfloat16)
+        low = (squares - high.astype(jnp.float32)).astype(jnp.bfloat16)
+        total = jnp.dot(high, same_head, preferred_element_type=jnp.float32) + jnp.dot(
+            low, same_head, preferred_element_type=jnp.float32
+        )
+        return part * lax.rsqrt(total * (1.0 / head_dim) + EPSILON)
+
+    size = same_line.shape[0]
+    mixtures = []
+    for start in range(0, tokens.shape[0], size):
+        projected = jnp.dot(tokens[start : start + size], w, preferred_element_type=jnp.float32)
+        queries = head_norm(projected[:, :LANES])
+        keys = head_norm(projected[:, LANES : 2 * LANES]).astype(jnp.bfloat16)
+        values = projected[:, 2 * LANES :]
+        parts = []
+        for head in range(2):
+            mine = first if head == 0 else jnp.logical_not(first)
+            query = jnp.where(mine, queries, 0.0).astype(jnp.bfloat16)
+            value = jnp.where(mine, values, 1.0).astype(jnp.bfloat16)
+            scores = lax.dot_general(
+                query, keys, (((1,), (1,)), ((), ())), preferred_element_type=jnp.float32
+            )
+            scores = jnp.where(same_line, scores * scales[head], MASKED)
+            weights = jnp.exp(scores - jnp.max(scores, axis=1, keepdims=True))
+            parts.append(
+                jnp.dot(weights.astype(jnp.bfloat16), value, preferred_element_type=jnp.float32)
+            )
+        mixed = jnp.where(first, parts[0], parts[1])
+        total = pltpu.roll(jnp.where(first, parts[1], parts[0]), LANES - head_dim, 1)
+        mixtures.append((mixed / total).astype(jnp.bfloat16))
+    return mixtures
+
+
+def line_masks(size, inner):
+    a = lax.broadcasted_iota(jnp.int32, (size, size), 0)
+    b = lax.broadcasted_iota(jnp.int32, (size, size), 1)
+    return lax.rem(a, inner) == lax.rem(b, inner), lax.div(a, inner) == lax.div(b, inner)
+
+
+def head_scales(scale_ref, branch, head_dim):
+    group = my_group()
+    return [scale_ref[branch, 2 * group + h] * (1.0 / math.sqrt(head_dim)) for h in range(2)]
+
+
+def y_kernel(head_dim, scale_ref, t0, t1, t2, t3, gain_ref, *refs):
+    piece_refs, out_ref, w_ref = refs[:-2], refs[-2], refs[-1]
+    place_weights(piece_refs, w_ref, 1)
+    chips, cells, channels = t0.shape
+    gain = gain_ref[...]
+    tokens = jnp.concatenate(
+        [normed_rows(t[...].reshape(chips * cells, channels), gain) for t in (t0, t1, t2, t3)], 0
+    )
+    same_inner, _ = line_masks(CORES * chips * cells, cells)
+    mixtures = attend(tokens, w_ref[0], head_scales(scale_ref, 1, head_dim), same_inner, head_dim)
+    for half, mixture in enumerate(mixtures):
+        split = mixture.reshape(CORES, chips, cells, LANES)
+        for core in range(CORES):
+            out_ref[:, core, half] = split[core]
+
+
+def place_out(keep_ref, came_ref, branch, w_ref):
+    me = lax.rem(lax.axis_index("xy"), 2 * CORES)
+    rows = keep_ref.shape[2]
+    for ref, flip in ((keep_ref, 0), (came_ref, 1)):
+        for side in range(2):
+            source = lax.bitwise_xor(me, 2 * side + flip)
+            w_ref[pl.ds(pl.multiple_of(source * rows, rows), rows), :] = ref[side, branch]
+
+
+def occupied_rows(pos_ref, gz_index, cells, tokens):
+    columns = pos_ref.shape[1] - 1
+    bits = jnp.int32(0)
+    for n in range(columns):
+        bit = lax.shift_left(jnp.int32(1), pos_ref[0, n])
+        bits = bits | jnp.where(n < pos_ref[0, columns], bit, 0)
+    x_local = tokens // cells
+    x = lax.broadcasted_iota(jnp.int32, (tokens, LANES), 0) // cells + gz_index * x_local
+    return lax.bitwise_and(lax.shift_right_logical(jnp.full_like(x, bits), x), 1) == 1
+
+
+def xz_kernel(head_dim, cells, scale_ref, pos_ref, other_ref, n0, n1, m0, m1, gain_ref, keep_ref,
+              came_ref, *refs):
+    piece_refs, out_ref, w_ref, back_ref = refs[:-3], refs[-3], refs[-2], refs[-1]
+    place_weights(piece_refs, w_ref, 2)
+    gain = gain_ref[...]
+    tokens = jnp.concatenate([normed_rows(t[...], gain) for t in (n0, n1, m0, m1)], 0)
+    size = n0.shape[0] * 2
+    same_inner, same_outer = line_masks(size, cells)
+    place_out(keep_ref, came_ref, 0, back_ref)
+    mixtures = attend(tokens, w_ref[0], head_scales(scale_ref, 0, head_dim), same_inner, head_dim)
+    for n, mixture in enumerate(mixtures):
+        out_ref[n * size : (n + 1) * size] = jnp.dot(
+            mixture, back_ref[...], preferred_element_type=jnp.float32
+        )
+    place_out(keep_ref, came_ref, 2, back_ref)
+    mixtures = attend(tokens, w_ref[1], head_scales(scale_ref, 2, head_dim), same_outer, head_dim)
+    half = lax.axis_index("gz")
+    for n, (mixture, ref) in enumerate(zip(mixtures, (pos_ref, other_ref))):
+        live = jnp.concatenate(
+            [occupied_rows(ref, half, cells, size // 2), occupied_rows(ref, 1 - half, cells, size // 2)], 0
+        )
+        mixture = jnp.where(live, mixture.astype(jnp.float32), 0.0).astype(jnp.bfloat16)
+        out_ref[n * size : (n + 1) * size] += jnp.dot(
+            mixture, back_ref[...], preferred_element_type=jnp.float32
+        )
+
+
+def out_kernel(mix_ref, keep_ref, came_ref, part_ref, own_ref, x_ref, c_ref, xc_ref, back_ref):
+    place_out(keep_ref, came_ref, 1, back_ref)
+    rows = own_ref.shape[0]
+    for core in range(CORES):
+        for half in range(2):
+            mixture = mix_ref[:, core, half].reshape(rows, LANES)
+            n = core * 2 + half
+            total = part_ref[n * rows : (n + 1) * rows] + jnp.dot(
+                mixture, back_ref[...], preferred_element_type=jnp.float32
+            )
+            ref = (own_ref, x_ref, c_ref, xc_ref)[n]
+            ref[...] = total.astype(ref.dtype)
+
+
+def vmem_call(kernel, scalars, arrays, out_shape, scratch, name, flops):
+    smem = pl.BlockSpec(memory_space=pltpu.SMEM)
+    vmem = pl.BlockSpec(memory_space=pltpu.VMEM)
+    moved = sum(a.size * a.dtype.itemsize for a in arrays)
+    return pl.pallas_call(
+        kernel,
+        out_shape=out_shape,
+        in_specs=[smem] * len(scalars) + [vmem] * len(arrays),
+        out_specs=jax.tree.map(lambda _: vmem, out_shape),
+        scratch_shapes=scratch,
+        name=name,
+        cost_estimate=pl.CostEstimate(flops=flops, bytes_accessed=moved, transcendentals=0),
+    )(*scalars, *arrays)
+
+
+def gather_tree(piece, bits, count):
+    pieces = [piece]
+    for bit in bits:
+        pieces = pieces + [xy_swap(p, bit, count) for p in pieces]
+    return pieces
+
+
+def grouped_shards(
+    n_xy,
+    hidden_features,
+    scaling_factors_prenormal,
+    attention_input_matrices,
+    final_projection_matrices,
+    score_scaling,
+    filled_pillar_positions,
+    filled_pillar_totals,
+):
+    x_local, z_cells, _, channels = hidden_features.shape
+    head_dim = channels // score_scaling.shape[1]
+    tokens = x_local * z_cells
+    chips = n_xy // CORES
+    me, half = lax.axis_index("xy"), lax.axis_index("gz")
+    same_core = [[k * CORES + c for k in range(chips)] for c in range(CORES)]
+    swap = functools.partial(xy_swap, count=n_xy)
+
+    own = hidden_features.reshape(tokens, channels)
+    y_own = lax.all_to_all(
+        own.reshape(chips, tokens // chips, channels), "xy", 0, 0, axis_index_groups=same_core, tiled=True
+    )
+    sliced = slice_weights(attention_input_matrices)
+
+    tree_bits = [1 << b for b in reversed(range(1, n_xy.bit_length() - 1))]
+    gathered = []
+    for chunk in range(len(BRANCH_CHUNKS)):
+        piece = jnp.stack([sliced[2 * chunk], swap(sliced[2 * chunk + 1], 1)])
+        gathered.append(gather_tree(piece, tree_bits, n_xy))
+    order = [0]
+    for bit in tree_bits:
+        order = order + [o | bit for o in order]
+    gathered = [[pieces[order.index(CORES * k)] for k in range(chips)] for pieces in gathered]
+
+    other = gz_swap(own)
+    y_other = gz_swap(y_own)
+    y_core, y_cross = swap(y_own, 1), swap(y_other, 1)
+    own_core, other_core = swap(own, 1), swap(other, 1)
+
+    top, low, side = n_xy // 2, n_xy // 4, n_xy // 8
+    pairs = []
+    for i in range(n_xy):
+        pairs += [(2 * i + h, 2 * (i ^ top) + h) for h in range(2) if i // top == h]
+    came = lax.ppermute(final_projection_matrices, ("xy", "gz"), pairs)
+    base = jnp.where(me // top == half, final_projection_matrices, came)
+    b, e, d, f = base, swap(base, side), None, None
+    d = swap(base, low)
+    f = swap(d, side)
+    is_low = lax.rem(me // low, 2) == lax.rem(me, CORES)
+    low_pair, high_pair = jnp.stack([b, e]), jnp.stack([d, f])
+    keep = jnp.where(is_low, low_pair, high_pair)
+    back = swap(jnp.where(is_low, high_pair, low_pair), 1)
+
+    columns = jnp.concatenate([filled_pillar_positions, filled_pillar_totals[:, None]], 1)
+    other_columns = swap(columns, 1)
+    gain = scaling_factors_prenormal[None, :]
+
+    per_branch = 2 * 4 * tokens * channels * 3 * LANES
+    y_mix = vmem_call(
+        functools.partial(y_kernel, head_dim),
+        [score_scaling],
+        [y_own, y_core, y_other, y_cross, gain] + gathered[0],
+        jax.ShapeDtypeStruct((chips, CORES, 2, z_cells, LANES), jnp.bfloat16),
+        [pltpu.VMEM((1, channels, 3 * LANES), jnp.bfloat16)],
+        "y_lines",
+        per_branch,
+    )
+    y_mix = lax.all_to_all(y_mix, "xy", 0, 0, axis_index_groups=same_core, tiled=True)
+    part = vmem_call(
+        functools.partial(xz_kernel, head_dim, z_cells),
+        [score_scaling, columns, other_columns],
+        [own, other, own_core, other_core, gain, keep, back] + gathered[1],
+        jax.ShapeDtypeStruct((4 * tokens, channels), jnp.float32),
+        [
+            pltpu.VMEM((2, channels, 3 * LANES), jnp.bfloat16),
+            pltpu.VMEM((LANES, channels), jnp.bfloat16),
+        ],
+        "xz_lines",
+        2 * per_branch,
+    )
+    send = jax.ShapeDtypeStruct((tokens, channels), jnp.bfloat16)
+    mine, to_gz, to_core, to_both = vmem_call(
+        out_kernel,
+        [],
+        [y_mix, keep, back, part],
+        [jax.ShapeDtypeStruct((tokens, channels), jnp.float32), send, send, send],
+        [pltpu.VMEM((LANES, channels), jnp.bfloat16)],
+        "y_out",
+        per_branch // 3,
+    )
+    both = [(2 * i + h, 2 * (i ^ 1) + 1 - h) for i in range(n_xy) for h in range(2)]
+    terms = [gz_swap(to_gz), swap(to_core, 1), lax.ppermute(to_both, ("xy", "gz"), both)]
+    total = own.astype(jnp.float32) + mine
+    for term in terms:
+        total = total + term.astype(jnp.float32)
+    return total.astype(jnp.bfloat16).reshape(hidden_features.shape)
+
+
+def can_group(mesh, hidden, w_back, scales, positions):
+    n_xy, n_gz = mesh.shape["xy"], mesh.shape["gz"]
+    x_local, z_cells, y_rows, channels = hidden
+    heads = scales[1]
+    groups = CORES * n_gz
+    return (
+        n_gz == 2
+        and n_xy == 4 * groups
+        and y_rows == 1
+        and x_local == n_xy // CORES
+        and z_cells % 16 == 0
+        and heads == 2 * groups
+        and channels == groups * LANES
+        and w_back[1] * n_xy == channels
+        and positions[1] == n_gz * x_local
+        and positions[1] <= 31
+    )
+
+
 def solution(mesh):
     in_specs = (
         P("gz", None, "xy", None),
@@ -144,4 +473,11 @@
         P("xy"),
     )
     out_specs = P("gz", None, "xy", None)
+
+    def shards(*args):
+        shapes = [a.shape for a in args]
+        if can_group(mesh, shapes[0], shapes[3], shapes[4], shapes[5]):
+            return grouped_shards(mesh.shape["xy"], *args)
+        return generic_shards(*args)
+
     return jax.shard_map(shards, mesh=mesh, in_specs=in_specs, out_specs=out_specs, check_vma=False)

time: 149 us -> 82.3 us (0.55)
  waiting for transfers between devices: 69.6 us -> 19.9 us
  starting transfers between devices: 24.1 us -> 40.6 us
  local copies, waits for them, and re-layouts: 19.2 us -> 3.41 us
  Pallas kernels: 0 us -> 14.2 us
  matrix products: 13.7 us -> 0 us
  between operations: 14.4 us -> 1.04 us
  other arithmetic: 7.31 us -> 2.51 us
    all_gather x2 -> x0, waiting for transfers between devices: 46 us -> none  [the longest x1 46 us: shards(): lax.all_gather(attention_input_matrices, 'xy', axis=1, tiled=True)]
    ppermute x0 -> x31, starting transfers between devices: none -> 29.6 us  [the longest x26 20.5 us: xy_swap(): return lax.ppermute(array, 'xy', [(i, i ^ bit) for i in range(count)])]
    all_to_all x6 -> x2, waiting for transfers between devices: 22.1 us -> 0.01 us  [the longest x1 0.01 us: grouped_shards(): lax.all_to_all(own.reshape(chips, tokens // chips, channels), 'xy', 0, 0,...]
    ppermute x0 -> x31, waiting for transfers between devices: none -> 19.9 us  [the longest x26 13.1 us: xy_swap(): return lax.ppermute(array, 'xy', [(i, i ^ bit) for i in range(count)])]
    pallas_call x0 -> x4, Pallas kernels: none -> 14.2 us  [the longest x3 12.6 us: vmem_call(): pl.pallas_call(kernel, out_shape=out_shape, in_specs=[smem] * len(scalars...]
    all_to_all x6 -> x2, starting transfers between devices: 24.1 us -> 11 us  [the longest x1 7.44 us: grouped_shards(): lax.all_to_all(own.reshape(chips, tokens // chips, channels), 'xy', 0, 0,...]
    dot_general x9 -> x0, matrix products: 10.4 us -> none  [the longest x3 4.68 us: project_qkv(): jnp.dot(tokens_in, w_project, preferred_element_type=jnp.float32)]
    dot_general x4 -> x0, local copies, waits for them, and re-layouts: 9.41 us -> none  [project_qkv(): jnp.dot(tokens_in, w_project, preferred_element_type=jnp.float32)]
  transfers between devices with their start and end apart: 8 -> 33, of which waited for: 7 -> 9; matrix products, arithmetic and copies ran while one was open for 25% -> 1% of each run, Pallas kernels for 0% -> 14%
where the time goes in v1:
time: 82.3 us; the launch traced here: 81.7 us
  starting transfers between devices  40.6 us (49%)
  waiting for transfers between devices  19.9 us (24%)
  Pallas kernels  14.2 us (17%)
  local copies, waits for them, and re-layouts  3.41 us (4%)
  other arithmetic  2.51 us (3%)
  between operations  1.04 us (1%)
    ppermute x26, starting transfers between devices, xy_swap(): return lax.ppermute(array, 'xy', [(i, i ^ bit) for i in range(count)])  20.5 us
    ppermute x26, waiting for transfers between devices, xy_swap(): return lax.ppermute(array, 'xy', [(i, i ^ bit) for i in range(count)])  13.1 us
    pallas_call x3, Pallas kernels, vmem_call(): pl.pallas_call(kernel, out_shape=out_shape, in_specs=[smem] * len(scalars...  12.6 us
    all_to_all x1, starting transfers between devices, grouped_shards(): lax.all_to_all(own.reshape(chips, tokens // chips, channels), 'xy', 0, 0,...  7.44 us
    ppermute x3, waiting for transfers between devices, gz_swap(): return lax.ppermute(array, 'gz', [(0, 1), (1, 0)])  5.02 us
    ppermute x1, starting transfers between devices, grouped_shards(): came = lax.ppermute(final_projection_matrices, ('xy', 'gz'), pairs)  4.82 us
    ppermute x3, starting transfers between devices, gz_swap(): return lax.ppermute(array, 'gz', [(0, 1), (1, 0)])  3.86 us
    all_to_all x1, starting transfers between devices, grouped_shards(): lax.all_to_all(y_mix, 'xy', 0, 0, axis_index_groups=same_core, tiled=True)  3.55 us
  transfers between devices with their start and end apart: 33, of which 9 were waited for; matrix products, arithmetic and copies ran while one was open for 1% of the time, Pallas kernels for 14%

profile of v1, /device:TPU:0, one launch (start us, length us, event | category | flops | bytes accessed | tf_op | source)
XLA Modules:
  0.0 81.7 jit_solution(15801407368635433403)
XLA Ops:
  0.0 7.4 %all-to-all-start = ((bf16[8,16,512]{2,1,0:T(8,128)(2,1)}), bf16[8,16,512]{2,1,0:T(8,128)(2,1)S(1)}, u32[]{:S(2)}, u32[]{:S(2)}) async-start(bf16[8,16,512]{2,1,0:T(8,128)(2,1)} %bitcast.17), calls=%async_computation | async-start | bytes 262144 | tf_op jit(solution)/shard_map/all_to_all | solution.py:367
  7.4 4.8 %collective-permute-start.11 = (bf16[3,32,512]{2,1,0:T(8,128)(2,1)S(1)}, bf16[3,32,512]{2,1,0:T(8,128)(2,1)S(1)}, u32[]{:S(2)}, u32[]{:S(2)}) collective-permute-start(bf16[3,32,512]{2,1,0:T(8,128)(2,1)S(1)} %copy-done.20), channel_id=1, source_target_pairs={{0,16},{2,18},{4,20},{6,22},{8,24},{10,26},{12,28},{14,30},{17,1},... | collective-permute-start | bytes 294920 | tf_op jit(solution)/shard_map/ppermute | solution.py:391
  12.3 1.6 %slice_weights.1 = (bf16[3,32,128]{2,1,0:T(8,128)(2,1)}, bf16[3,32,128]{2,1,0:T(8,128)(2,1)}, bf16[6,32,128]{2,1,0:T(8,128)(2,1)}, bf16[6,32,128]{2,1,0:T(8,128)(2,1)}) custom-call(bf16[3,32,1536]{2,1,0:T(8,128)(2,1)} %w_ref.1), custom_call_target="tpu_custom_call" | custom-call | tf_op jit(solution)/shard_map/slice_weights/pallas_call | solution.py:181
  13.9 0.5 collective-permute-start.3
  15.1 0.6 copy-done.32
  15.7 0.1 pad_add_fusion.pos_ref
  15.8 0.5 copy-done.30
  16.3 0.2 copy-done.29
  16.6 0.1 collective-permute-start.7
  16.7 1.5 %collective-permute-start.5 = (bf16[2,3,32,128]{3,2,1,0:T(8,128)(2,1)S(1)}, bf16[2,3,32,128]{3,2,1,0:T(8,128)(2,1)S(1)}, u32[]{:S(2)}, u32[]{:S(2)}) collective-permute-start(bf16[2,3,32,128]{3,2,1,0:T(8,128)(2,1)S(1)} %pad_maximum_fusion.3.refs_0_), channel_id=1, source_target_pairs={{0,8},{2,10},{4,12},{6,14},{8,0},{10,2},{12,4},{14,6},{16,24},{18,... | collective-permute-start | bytes 147464 | tf_op jit(solution)/shard_map/ppermute | solution.py:146
  18.2 2.1 %collective-permute-start.1 = (bf16[8,16,512]{2,1,0:T(8,128)(2,1)S(1)}, bf16[8,16,512]{2,1,0:T(8,128)(2,1)S(1)}, u32[]{:S(2)}, u32[]{:S(2)}) collective-permute-start(bf16[8,16,512]{2,1,0:T(8,128)(2,1)S(1)} %all-to-all-done.t0), channel_id=1, source_target_pairs={{0,1},{1,0},{2,3},{3,2},{4,5},{5,4},{6,7},{7,6},{8,9},{9,8},{10,11... | collective-permute-start | bytes 393224 | tf_op jit(solution)/shard_map/ppermute | solution.py:150
  20.3 0.1 collective-permute-start.13
  20.4 2.0 %collective-permute-start.4 = (bf16[2,3,32,128]{3,2,1,0:T(8,128)(2,1)S(1)}, bf16[2,3,32,128]{3,2,1,0:T(8,128)(2,1)S(1)}, u32[]{:S(2)}, u32[]{:S(2)}) collective-permute-start(bf16[2,3,32,128]{3,2,1,0:T(8,128)(2,1)S(1)} %pad_maximum_fusion.3.refs_0_), channel_id=1, source_target_pairs={{0,4},{2,6},{4,0},{6,2},{8,12},{10,14},{12,8},{14,10},{16,20},{18,... | collective-permute-start | bytes 147464 | tf_op jit(solution)/shard_map/ppermute | solution.py:146
  22.4 1.5 %collective-permute-start.9 = (bf16[2,3,32,128]{3,2,1,0:T(8,128)(2,1)S(1)}, bf16[2,3,32,128]{3,2,1,0:T(8,128)(2,1)S(1)}, u32[]{:S(2)}, u32[]{:S(2)}) collective-permute-start(bf16[2,3,32,128]{3,2,1,0:T(8,128)(2,1)S(1)} %collective-permute-done.7.refs_4_), channel_id=1, source_target_pairs={{0,8},{2,10},{4,12},{6,14},{8,0},{10,2},{12,4},{14,6},{16,24},{18,... | collective-permute-start | bytes 147464 | tf_op jit(solution)/shard_map/ppermute | solution.py:146
  23.8 0.8 collective-permute-start.8
  24.7 2.2 %collective-permute-start.6 = (bf16[2,3,32,128]{3,2,1,0:T(8,128)(2,1)S(1)}, bf16[2,3,32,128]{3,2,1,0:T(8,128)(2,1)S(1)}, u32[]{:S(2)}, u32[]{:S(2)}) collective-permute-start(bf16[2,3,32,128]{3,2,1,0:T(8,128)(2,1)S(1)} %collective-permute-done.5.refs_2_), channel_id=1, source_target_pairs={{0,4},{2,6},{4,0},{6,2},{8,12},{10,14},{12,8},{14,10},{16,20},{18,... | collective-permute-start | bytes 147464 | tf_op jit(solution)/shard_map/ppermute | solution.py:146
  27.0 1.1 %collective-permute-done.8.refs_5_ = bf16[2,3,32,128]{3,2,1,0:T(8,128)(2,1)S(1)} collective-permute-done((bf16[2,3,32,128]{3,2,1,0:T(8,128)(2,1)S(1)}, bf16[2,3,32,128]{3,2,1,0:T(8,128)(2,1)S(1)}, u32[]{:S(2)}, u32[]{:S(2)}) %collective-permute-start.8) | collective-permute-done | bytes 49184 | tf_op jit(solution)/shard_map/ppermute | solution.py:146
  28.0 0.7 collective-permute-start.12
  28.8 1.3 %collective-permute-start.14 = (bf16[3,32,512]{2,1,0:T(8,128)(2,1)S(1)}, bf16[3,32,512]{2,1,0:T(8,128)(2,1)S(1)}, u32[]{:S(2)}, u32[]{:S(2)}) collective-permute-start(bf16[3,32,512]{2,1,0:T(8,128)(2,1)S(1)} %collective-permute-done.13), channel_id=1, source_target_pairs={{0,4},{2,6},{4,0},{6,2},{8,12},{10,14},{12,8},{14,10},{16,20},{18,... | collective-permute-start | bytes 294920 | tf_op jit(solution)/shard_map/ppermute | solution.py:146
  30.1 0.5 collective-permute-start.2
  30.7 1.2 %collective-permute-done.17.n1 = bf16[128,512]{1,0:T(8,128)(2,1)S(1)} collective-permute-done((bf16[128,512]{1,0:T(8,128)(2,1)S(1)}, bf16[128,512]{1,0:T(8,128)(2,1)S(1)}, u32[]{:S(2)}, u32[]{:S(2)}) %collective-permute-start.17) | collective-permute-done | bytes 131104 | tf_op jit(solution)/shard_map/ppermute | solution.py:150
  31.9 0.7 collective-permute-done.12
  32.6 1.7 %collective-permute-start.24 = (bf16[2,6,32,128]{3,2,1,0:T(8,128)(2,1)S(1)}, bf16[2,6,32,128]{3,2,1,0:T(8,128)(2,1)S(1)}, u32[]{:S(2)}, u32[]{:S(2)}) collective-permute-start(bf16[2,6,32,128]{3,2,1,0:T(8,128)(2,1)S(1)} %pad_maximum_fusion.2.refs_0_), channel_id=1, source_target_pairs={{0,16},{2,18},{4,20},{6,22},{8,24},{10,26},{12,28},{14,30},{16,0},... | collective-permute-start | bytes 294920 | tf_op jit(solution)/shard_map/ppermute | solution.py:146
  34.4 0.5 collective-permute-start.10
  34.9 0.7 broadcast_select_fusion
  35.6 4.5 %collective-permute-done.24.refs_4_ = bf16[2,6,32,128]{3,2,1,0:T(8,128)(2,1)S(1)} collective-permute-done((bf16[2,6,32,128]{3,2,1,0:T(8,128)(2,1)S(1)}, bf16[2,6,32,128]{3,2,1,0:T(8,128)(2,1)S(1)}, u32[]{:S(2)}, u32[]{:S(2)}) %collective-permute-start.24) | collective-permute-done | bytes 98336 | tf_op jit(solution)/shard_map/ppermute | solution.py:146
  40.1 0.9 %collective-permute-start.21 = (bf16[2,6,32,128]{3,2,1,0:T(8,128)(2,1)S(1)}, bf16[2,6,32,128]{3,2,1,0:T(8,128)(2,1)S(1)}, u32[]{:S(2)}, u32[]{:S(2)}) collective-permute-start(bf16[2,6,32,128]{3,2,1,0:T(8,128)(2,1)S(1)} %pad_maximum_fusion.2.refs_0_), channel_id=1, source_target_pairs={{0,4},{2,6},{4,0},{6,2},{8,12},{10,14},{12,8},{14,10},{16,20},{18,... | collective-permute-start | bytes 294920 | tf_op jit(solution)/shard_map/ppermute | solution.py:146
  41.1 2.0 %collective-permute-start.26 = (bf16[2,6,32,128]{3,2,1,0:T(8,128)(2,1)S(1)}, bf16[2,6,32,128]{3,2,1,0:T(8,128)(2,1)S(1)}, u32[]{:S(2)}, u32[]{:S(2)}) collective-permute-start(bf16[2,6,32,128]{3,2,1,0:T(8,128)(2,1)S(1)} %collective-permute-done.24.refs_4_), channel_id=1, source_target_pairs={{0,8},{2,10},{4,12},{6,14},{8,0},{10,2},{12,4},{14,6},{16,24},{18,... | collective-permute-start | bytes 294920 | tf_op jit(solution)/shard_map/ppermute | solution.py:146
  43.1 0.6 copy-done.12
  43.8 3.7 %y_lines.1 = bf16[8,2,2,16,128]{4,3,2,1,0:T(8,128)(2,1)} custom-call(f32[3,8]{1,0:T(4,128)} %scale_ref.3, bf16[8,16,512]{2,1,0:T(8,128)(2,1)} %copy-done.4, bf16[8,16,512]{2,1,0:T(8,128)(2,1)} %copy-done.11, bf16[8,16,512]{2,1,0:T(8,128)(2,1)} %copy-done.10, bf16[8,16,512]{2,1,0:T(8,128)(2,1)} %copy-done.12, f32[1,512]{1,0:T(1,128)} %bitcast.29, ...), custom_call_target="tpu_custom_call" | custom-call | flops 201326592 | bytes 919552 | tf_op jit(solution)/shard_map/y_lines/pallas_call | solution.py:330
  47.5 3.6 %all-to-all-start.1 = ((bf16[8,2,2,16,128]{4,3,2,1,0:T(8,128)(2,1)}), bf16[8,2,2,16,128]{4,3,2,1,0:T(8,128)(2,1)S(1)}, u32[]{:S(2)}, u32[]{:S(2)}) async-start(bf16[8,2,2,16,128]{4,3,2,1,0:T(8,128)(2,1)} %y_lines.1), calls=%async_computation.1 | async-start | bytes 262144 | tf_op jit(solution)/shard_map/all_to_all | solution.py:415
  51.0 0.1 collective-permute-start.19
  51.2 2.1 %collective-permute-start.25 = (bf16[2,6,32,128]{3,2,1,0:T(8,128)(2,1)S(1)}, bf16[2,6,32,128]{3,2,1,0:T(8,128)(2,1)S(1)}, u32[]{:S(2)}, u32[]{:S(2)}) collective-permute-start(bf16[2,6,32,128]{3,2,1,0:T(8,128)(2,1)S(1)} %collective-permute-done.24.refs_4_), channel_id=1, source_target_pairs={{0,4},{2,6},{4,0},{6,2},{8,12},{10,14},{12,8},{14,10},{16,20},{18,... | collective-permute-start | bytes 294920 | tf_op jit(solution)/shard_map/ppermute | solution.py:146
  53.2 0.1 collective-permute-start.23
  53.3 1.9 %collective-permute-start.27 = (bf16[2,6,32,128]{3,2,1,0:T(8,128)(2,1)S(1)}, bf16[2,6,32,128]{3,2,1,0:T(8,128)(2,1)S(1)}, u32[]{:S(2)}, u32[]{:S(2)}) collective-permute-start(bf16[2,6,32,128]{3,2,1,0:T(8,128)(2,1)S(1)} %collective-permute-done.26.refs_6_), channel_id=1, source_target_pairs={{0,4},{2,6},{4,0},{6,2},{8,12},{10,14},{12,8},{14,10},{16,20},{18,... | collective-permute-start | bytes 294920 | tf_op jit(solution)/shard_map/ppermute | solution.py:146
  55.3 2.7 %collective-permute-done.25.refs_5_ = bf16[2,6,32,128]{3,2,1,0:T(8,128)(2,1)S(1)} collective-permute-done((bf16[2,6,32,128]{3,2,1,0:T(8,128)(2,1)S(1)}, bf16[2,6,32,128]{3,2,1,0:T(8,128)(2,1)S(1)}, u32[]{:S(2)}, u32[]{:S(2)}) %collective-permute-start.25) | collective-permute-done | bytes 98336 | tf_op jit(solution)/shard_map/ppermute | solution.py:146
  57.9 2.3 %collective-permute-done.23.refs_3_ = bf16[2,6,32,128]{3,2,1,0:T(8,128)(2,1)S(1)} collective-permute-done((bf16[2,6,32,128]{3,2,1,0:T(8,128)(2,1)S(1)}, bf16[2,6,32,128]{3,2,1,0:T(8,128)(2,1)S(1)}, u32[]{:S(2)}, u32[]{:S(2)}) %collective-permute-start.23) | collective-permute-done | bytes 98336 | tf_op jit(solution)/shard_map/ppermute | solution.py:146
  60.2 1.8 %collective-permute-done.27.refs_7_ = bf16[2,6,32,128]{3,2,1,0:T(8,128)(2,1)S(1)} collective-permute-done((bf16[2,6,32,128]{3,2,1,0:T(8,128)(2,1)S(1)}, bf16[2,6,32,128]{3,2,1,0:T(8,128)(2,1)S(1)}, u32[]{:S(2)}, u32[]{:S(2)}) %collective-permute-start.27) | collective-permute-done | bytes 98336 | tf_op jit(solution)/shard_map/ppermute | solution.py:146
  62.1 0.6 copy-done.19
  62.7 0.1 copy-done.2
  62.8 6.3 %xz_lines.1.part_ref = f32[512,512]{1,0:T(8,128)} custom-call(f32[3,8]{1,0:T(4,128)} %scale_ref.3, s32[1,17]{1,0:T(1,128)} %copy-done.30, s32[1,17]{1,0:T(1,128)} %copy-done.31, bf16[128,512]{1,0:T(8,128)(2,1)} %bitcast.18, bf16[128,512]{1,0:T(8,128)(2,1)} %copy-done.7, bf16[128,512]{1,0:T(8,128)(2,1)} %copy-done.8, bf16[128,512]{1,0:T(8,128)(2,1)} %copy-done.9, ...), custom_call_target="tpu_custom_call" | custom-call | flops 402653184 | bytes 1705984 | tf_op jit(solution)/shard_map/xz_lines/pallas_call | solution.py:330
  69.1 0.6 copy-done.3
  69.7 2.6 %y_out.1 = (f32[128,512]{1,0:T(8,128)}, bf16[128,512]{1,0:T(8,128)(2,1)}, bf16[128,512]{1,0:T(8,128)(2,1)}, bf16[128,512]{1,0:T(8,128)(2,1)}) custom-call(bf16[8,2,2,16,128]{4,3,2,1,0:T(8,128)(2,1)} %copy-done.3, bf16[2,3,32,512]{3,2,1,0:T(8,128)(2,1)} %get-tuple-element.22.keep_ref, bf16[2,3,32,512]{3,2,1,0:T(8,128)(2,1)} %copy-done.2, ...), custom_call_target="tpu_custom_call" | custom-call | flops 67108864 | bytes 1572864 | tf_op jit(solution)/shard_map/y_out/pallas_call | solution.py:330
  72.3 1.7 %collective-permute-start.28 = (bf16[128,512]{1,0:T(8,128)(2,1)}, bf16[128,512]{1,0:T(8,128)(2,1)S(1)}, u32[]{:S(2)}, u32[]{:S(2)}) collective-permute-start(bf16[128,512]{1,0:T(8,128)(2,1)} %get-tuple-element.18), channel_id=1, source_target_pairs={{0,1},{1,0},{2,3},{3,2},{4,5},{5,4},{6,7},{7,6},{8,9},{9,8},{10,11... | collective-permute-start | bytes 393224 | tf_op jit(solution)/shard_map/ppermute | solution.py:150
  74.0 0.4 collective-permute-start.30
  74.4 3.8 %collective-permute-done.28 = bf16[128,512]{1,0:T(8,128)(2,1)S(1)} collective-permute-done((bf16[128,512]{1,0:T(8,128)(2,1)}, bf16[128,512]{1,0:T(8,128)(2,1)S(1)}, u32[]{:S(2)}, u32[]{:S(2)}) %collective-permute-start.28) | collective-permute-done | bytes 131104 | tf_op jit(solution)/shard_map/ppermute | solution.py:150
  78.3 1.8 %collective-permute-done.30 = bf16[128,512]{1,0:T(8,128)(2,1)S(1)} collective-permute-done((bf16[128,512]{1,0:T(8,128)(2,1)}, bf16[128,512]{1,0:T(8,128)(2,1)S(1)}, u32[]{:S(2)}, u32[]{:S(2)}) %collective-permute-start.30) | collective-permute-done | bytes 131104 | tf_op jit(solution)/shard_map/ppermute | solution.py:439
  80.0 1.7 %add_convert_fusion = bf16[128,512]{1,0:T(8,128)(2,1)} fusion(bf16[128,512]{1,0:T(8,128)(2,1)S(1)} %collective-permute-done.30, bf16[128,512]{1,0:T(8,128)(2,1)S(1)} %collective-permute-done.29, bf16[128,512]{1,0:T(8,128)(2,1)S(1)} %collective-permute-done.28, f32[128,512]{1,0:T(8,128)} %get-tuple-element.17, bf16[8,16,1,512]{3,1,2,0:T(8,128)(2,1)S(1)} %copy-done.1), kind=kLoop, calls=%fused_computation | loop fusion | flops 589824 | bytes 917504 | tf_op jit(solution)/shard_map/convert_element_type | solution.py:443
  (94 shorter events, 0.4 us)
Async XLA Ops:
  0.0 7.4 %copy-start.20 = (bf16[3,32,512]{2,1,0:T(8,128)(2,1)S(1)}, bf16[3,32,512]{2,1,0:T(8,128)(2,1)}, u32[]{:S(2)}) copy-start(bf16[3,32,512]{2,1,0:T(8,128)(2,1)} %param.10) | copy-start | bytes 294916
  0.0 18.2 %all-to-all-start = ((bf16[8,16,512]{2,1,0:T(8,128)(2,1)}), bf16[8,16,512]{2,1,0:T(8,128)(2,1)S(1)}, u32[]{:S(2)}, u32[]{:S(2)}) async-start(bf16[8,16,512]{2,1,0:T(8,128)(2,1)} %bitcast.17), calls=%async_computation | async-start | bytes 262144 | tf_op jit(solution)/shard_map/all_to_all | solution.py:367
  7.4 10.7 %collective-permute-start.11 = (bf16[3,32,512]{2,1,0:T(8,128)(2,1)S(1)}, bf16[3,32,512]{2,1,0:T(8,128)(2,1)S(1)}, u32[]{:S(2)}, u32[]{:S(2)}) collective-permute-start(bf16[3,32,512]{2,1,0:T(8,128)(2,1)S(1)} %copy-done.20), channel_id=1, source_target_pairs={{0,16},{2,18},{4,20},{6,22},{8,24},{10,26},{12,28},{14,30},{17,1},... | collective-permute-start | bytes 294920 | tf_op jit(solution)/shard_map/ppermute | solution.py:391
  13.9 6.5 %collective-permute-start.20 = (bf16[6,32,128]{2,1,0:T(8,128)(2,1)}, bf16[6,32,128]{2,1,0:T(8,128)(2,1)S(1)}, u32[]{:S(2)}, u32[]{:S(2)}) collective-permute-start(bf16[6,32,128]{2,1,0:T(8,128)(2,1)} %get-tuple-element.16), channel_id=1, source_target_pairs={{0,2},{2,0},{4,6},{6,4},{8,10},{10,8},{12,14},{14,12},{16,18},{18,... | collective-permute-start | bytes 147464 | tf_op jit(solution)/shard_map/ppermute | solution.py:146
  13.9 2.4 %collective-permute-start.3 = (bf16[3,32,128]{2,1,0:T(8,128)(2,1)}, bf16[3,32,128]{2,1,0:T(8,128)(2,1)S(1)}, u32[]{:S(2)}, u32[]{:S(2)}) collective-permute-start(bf16[3,32,128]{2,1,0:T(8,128)(2,1)} %get-tuple-element.14), channel_id=1, source_target_pairs={{0,2},{2,0},{4,6},{6,4},{8,10},{10,8},{12,14},{14,12},{16,18},{18,... | collective-permute-start | bytes 73736 | tf_op jit(solution)/shard_map/ppermute | solution.py:146
  15.8 4.5 %collective-permute-start.16 = (s32[1,17]{1,0:T(1,128)S(1)}, s32[1,17]{1,0:T(1,128)S(1)}, u32[]{:S(2)}, u32[]{:S(2)}) collective-permute-start(s32[1,17]{1,0:T(1,128)S(1)} %pad_add_fusion.pos_ref), channel_id=1, source_target_pairs={{0,2},{2,0},{4,6},{6,4},{8,10},{10,8},{12,14},{14,12},{16,18},{18,... | collective-permute-start | bytes 212 | tf_op jit(solution)/shard_map/ppermute | solution.py:146
  16.6 10.3 %copy-start = (bf16[8,16,1,512]{3,1,2,0:T(8,128)(2,1)S(1)}, bf16[8,16,1,512]{3,1,2,0:T(8,128)(2,1)}, u32[]{:S(2)}) copy-start(bf16[8,16,1,512]{3,1,2,0:T(8,128)(2,1)} %param.7) | copy-start | bytes 393220
  16.6 5.8 %collective-permute-start.7 = (bf16[2,3,32,128]{3,2,1,0:T(8,128)(2,1)S(1)}, bf16[2,3,32,128]{3,2,1,0:T(8,128)(2,1)S(1)}, u32[]{:S(2)}, u32[]{:S(2)}) collective-permute-start(bf16[2,3,32,128]{3,2,1,0:T(8,128)(2,1)S(1)} %pad_maximum_fusion.3.refs_0_), channel_id=1, source_target_pairs={{0,16},{2,18},{4,20},{6,22},{8,24},{10,26},{12,28},{14,30},{16,0},... | collective-permute-start | bytes 147464 | tf_op jit(solution)/shard_map/ppermute | solution.py:146
  16.7 7.2 %collective-permute-start.5 = (bf16[2,3,32,128]{3,2,1,0:T(8,128)(2,1)S(1)}, bf16[2,3,32,128]{3,2,1,0:T(8,128)(2,1)S(1)}, u32[]{:S(2)}, u32[]{:S(2)}) collective-permute-start(bf16[2,3,32,128]{3,2,1,0:T(8,128)(2,1)S(1)} %pad_maximum_fusion.3.refs_0_), channel_id=1, source_target_pairs={{0,8},{2,10},{4,12},{6,14},{8,0},{10,2},{12,4},{14,6},{16,24},{18,... | collective-permute-start | bytes 147464 | tf_op jit(solution)/shard_map/ppermute | solution.py:146
  18.2 11.9 %copy-start.4 = (bf16[8,16,512]{2,1,0:T(8,128)(2,1)}, bf16[8,16,512]{2,1,0:T(8,128)(2,1)S(1)}, u32[]{:S(2)}) copy-start(bf16[8,16,512]{2,1,0:T(8,128)(2,1)S(1)} %all-to-all-done.t0) | copy-start | bytes 393220
  18.2 11.9 %collective-permute-start.1 = (bf16[8,16,512]{2,1,0:T(8,128)(2,1)S(1)}, bf16[8,16,512]{2,1,0:T(8,128)(2,1)S(1)}, u32[]{:S(2)}, u32[]{:S(2)}) collective-permute-start(bf16[8,16,512]{2,1,0:T(8,128)(2,1)S(1)} %all-to-all-done.t0), channel_id=1, source_target_pairs={{0,1},{1,0},{2,3},{3,2},{4,5},{5,4},{6,7},{7,6},{8,9},{9,8},{10,11... | collective-permute-start | bytes 393224 | tf_op jit(solution)/shard_map/ppermute | solution.py:150
  20.3 10.4 %copy-start.28 = (bf16[6,32,128]{2,1,0:T(8,128)(2,1)S(1)}, bf16[6,32,128]{2,1,0:T(8,128)(2,1)}, u32[]{:S(2)}) copy-start(bf16[6,32,128]{2,1,0:T(8,128)(2,1)} %get-tuple-element.15) | copy-start | bytes 147460
  20.3 8.4 %collective-permute-start.13 = (bf16[3,32,512]{2,1,0:T(8,128)(2,1)S(1)}, bf16[3,32,512]{2,1,0:T(8,128)(2,1)S(1)}, u32[]{:S(2)}, u32[]{:S(2)}) collective-permute-start(bf16[3,32,512]{2,1,0:T(8,128)(2,1)S(1)} %broadcast_select_fusion.2), channel_id=1, source_target_pairs={{0,8},{2,10},{4,12},{6,14},{8,0},{10,2},{12,4},{14,6},{16,24},{18,... | collective-permute-start | bytes 294920 | tf_op jit(solution)/shard_map/ppermute | solution.py:146
  20.4 4.2 %collective-permute-start.4 = (bf16[2,3,32,128]{3,2,1,0:T(8,128)(2,1)S(1)}, bf16[2,3,32,128]{3,2,1,0:T(8,128)(2,1)S(1)}, u32[]{:S(2)}, u32[]{:S(2)}) collective-permute-start(bf16[2,3,32,128]{3,2,1,0:T(8,128)(2,1)S(1)} %pad_maximum_fusion.3.refs_0_), channel_id=1, source_target_pairs={{0,4},{2,6},{4,0},{6,2},{8,12},{10,14},{12,8},{14,10},{16,20},{18,... | collective-permute-start | bytes 147464 | tf_op jit(solution)/shard_map/ppermute | solution.py:146
  22.4 8.3 %copy-start.21 = (bf16[2,3,32,128]{3,2,1,0:T(8,128)(2,1)}, bf16[2,3,32,128]{3,2,1,0:T(8,128)(2,1)S(1)}, u32[]{:S(2)}) copy-start(bf16[2,3,32,128]{3,2,1,0:T(8,128)(2,1)S(1)} %collective-permute-done.7.refs_4_) | copy-start | bytes 147460
  22.4 4.5 %collective-permute-start.9 = (bf16[2,3,32,128]{3,2,1,0:T(8,128)(2,1)S(1)}, bf16[2,3,32,128]{3,2,1,0:T(8,128)(2,1)S(1)}, u32[]{:S(2)}, u32[]{:S(2)}) collective-permute-start(bf16[2,3,32,128]{3,2,1,0:T(8,128)(2,1)S(1)} %collective-permute-done.7.refs_4_), channel_id=1, source_target_pairs={{0,8},{2,10},{4,12},{6,14},{8,0},{10,2},{12,4},{14,6},{16,24},{18,... | collective-permute-start | bytes 147464 | tf_op jit(solution)/shard_map/ppermute | solution.py:146
  23.8 4.2 %collective-permute-start.8 = (bf16[2,3,32,128]{3,2,1,0:T(8,128)(2,1)S(1)}, bf16[2,3,32,128]{3,2,1,0:T(8,128)(2,1)S(1)}, u32[]{:S(2)}, u32[]{:S(2)}) collective-permute-start(bf16[2,3,32,128]{3,2,1,0:T(8,128)(2,1)S(1)} %collective-permute-done.7.refs_4_), channel_id=1, source_target_pairs={{0,4},{2,6},{4,0},{6,2},{8,12},{10,14},{12,8},{14,10},{16,20},{18,... | collective-permute-start | bytes 147464 | tf_op jit(solution)/shard_map/ppermute | solution.py:146
  24.7 5.4 %collective-permute-start.6 = (bf16[2,3,32,128]{3,2,1,0:T(8,128)(2,1)S(1)}, bf16[2,3,32,128]{3,2,1,0:T(8,128)(2,1)S(1)}, u32[]{:S(2)}, u32[]{:S(2)}) collective-permute-start(bf16[2,3,32,128]{3,2,1,0:T(8,128)(2,1)S(1)} %collective-permute-done.5.refs_2_), channel_id=1, source_target_pairs={{0,4},{2,6},{4,0},{6,2},{8,12},{10,14},{12,8},{14,10},{16,20},{18,... | collective-permute-start | bytes 147464 | tf_op jit(solution)/shard_map/ppermute | solution.py:146
  26.8 7.5 %copy-start.24 = (bf16[2,3,32,128]{3,2,1,0:T(8,128)(2,1)}, bf16[2,3,32,128]{3,2,1,0:T(8,128)(2,1)S(1)}, u32[]{:S(2)}) copy-start(bf16[2,3,32,128]{3,2,1,0:T(8,128)(2,1)S(1)} %collective-permute-done.9.refs_6_) | copy-start | bytes 147460
  26.9 5.0 %collective-permute-start.17 = (bf16[128,512]{1,0:T(8,128)(2,1)S(1)}, bf16[128,512]{1,0:T(8,128)(2,1)S(1)}, u32[]{:S(2)}, u32[]{:S(2)}) collective-permute-start(bf16[128,512]{1,0:T(8,128)(2,1)S(1)} %bitcast.19), channel_id=1, source_target_pairs={{0,1},{1,0},{2,3},{3,2},{4,5},{5,4},{6,7},{7,6},{8,9},{9,8},{10,11... | collective-permute-start | bytes 393224 | tf_op jit(solution)/shard_map/ppermute | solution.py:150
  28.0 7.6 %copy-start.25 = (bf16[2,3,32,128]{3,2,1,0:T(8,128)(2,1)}, bf16[2,3,32,128]{3,2,1,0:T(8,128)(2,1)S(1)}, u32[]{:S(2)}) copy-start(bf16[2,3,32,128]{3,2,1,0:T(8,128)(2,1)S(1)} %collective-permute-done.8.refs_5_) | copy-start | bytes 147460
  28.0 4.6 %collective-permute-start.12 = (bf16[3,32,512]{2,1,0:T(8,128)(2,1)S(1)}, bf16[3,32,512]{2,1,0:T(8,128)(2,1)S(1)}, u32[]{:S(2)}, u32[]{:S(2)}) collective-permute-start(bf16[3,32,512]{2,1,0:T(8,128)(2,1)S(1)} %broadcast_select_fusion.2), channel_id=1, source_target_pairs={{0,4},{2,6},{4,0},{6,2},{8,12},{10,14},{12,8},{14,10},{16,20},{18,... | collective-permute-start | bytes 294920 | tf_op jit(solution)/shard_map/ppermute | solution.py:146
  28.8 5.6 %collective-permute-start.14 = (bf16[3,32,512]{2,1,0:T(8,128)(2,1)S(1)}, bf16[3,32,512]{2,1,0:T(8,128)(2,1)S(1)}, u32[]{:S(2)}, u32[]{:S(2)}) collective-permute-start(bf16[3,32,512]{2,1,0:T(8,128)(2,1)S(1)} %collective-permute-done.13), channel_id=1, source_target_pairs={{0,4},{2,6},{4,0},{6,2},{8,12},{10,14},{12,8},{14,10},{16,20},{18,... | collective-permute-start | bytes 294920 | tf_op jit(solution)/shard_map/ppermute | solution.py:146
  30.1 11.0 %collective-permute-start = (bf16[8,16,512]{2,1,0:T(8,128)(2,1)S(1)}, bf16[8,16,512]{2,1,0:T(8,128)(2,1)S(1)}, u32[]{:S(2)}, u32[]{:S(2)}) collective-permute-start(bf16[8,16,512]{2,1,0:T(8,128)(2,1)S(1)} %all-to-all-done.t0), channel_id=1, source_target_pairs={{0,2},{2,0},{4,6},{6,4},{8,10},{10,8},{12,14},{14,12},{16,18},{18,... | collective-permute-start | bytes 393224 | tf_op jit(solution)/shard_map/ppermute | solution.py:146
  30.1 12.9 %collective-permute-start.2 = (bf16[8,16,512]{2,1,0:T(8,128)(2,1)S(1)}, bf16[8,16,512]{2,1,0:T(8,128)(2,1)S(1)}, u32[]{:S(2)}, u32[]{:S(2)}) collective-permute-start(bf16[8,16,512]{2,1,0:T(8,128)(2,1)S(1)} %collective-permute-done.1.t2), channel_id=1, source_target_pairs={{0,2},{2,0},{4,6},{6,4},{8,10},{10,8},{12,14},{14,12},{16,18},{18,... | collective-permute-start | bytes 393224 | tf_op jit(solution)/shard_map/ppermute | solution.py:146
  30.7 9.4 %copy-start.5 = (bf16[2,6,32,128]{3,2,1,0:T(8,128)(2,1)}, bf16[2,6,32,128]{3,2,1,0:T(8,128)(2,1)S(1)}, u32[]{:S(2)}) copy-start(bf16[2,6,32,128]{3,2,1,0:T(8,128)(2,1)S(1)} %pad_maximum_fusion.2.refs_0_) | copy-start | bytes 294916
  31.9 19.1 %copy-start.7 = (bf16[128,512]{1,0:T(8,128)(2,1)}, bf16[128,512]{1,0:T(8,128)(2,1)S(1)}, u32[]{:S(2)}) copy-start(bf16[128,512]{1,0:T(8,128)(2,1)S(1)} %collective-permute-done.17.n1) | copy-start | bytes 393220
  31.9 19.1 %collective-permute-start.18 = (bf16[128,512]{1,0:T(8,128)(2,1)S(1)}, bf16[128,512]{1,0:T(8,128)(2,1)S(1)}, u32[]{:S(2)}, u32[]{:S(2)}) collective-permute-start(bf16[128,512]{1,0:T(8,128)(2,1)S(1)} %bitcast.20), channel_id=1, source_target_pairs={{0,2},{2,0},{4,6},{6,4},{8,10},{10,8},{12,14},{14,12},{16,18},{18,... | collective-permute-start | bytes 393224 | tf_op jit(solution)/shard_map/ppermute | solution.py:146
  32.6 7.5 %collective-permute-start.24 = (bf16[2,6,32,128]{3,2,1,0:T(8,128)(2,1)S(1)}, bf16[2,6,32,128]{3,2,1,0:T(8,128)(2,1)S(1)}, u32[]{:S(2)}, u32[]{:S(2)}) collective-permute-start(bf16[2,6,32,128]{3,2,1,0:T(8,128)(2,1)S(1)} %pad_maximum_fusion.2.refs_0_), channel_id=1, source_target_pairs={{0,16},{2,18},{4,20},{6,22},{8,24},{10,26},{12,28},{14,30},{16,0},... | collective-permute-start | bytes 294920 | tf_op jit(solution)/shard_map/ppermute | solution.py:146
  34.4 5.8 %collective-permute-start.10 = (bf16[2,3,32,128]{3,2,1,0:T(8,128)(2,1)S(1)}, bf16[2,3,32,128]{3,2,1,0:T(8,128)(2,1)S(1)}, u32[]{:S(2)}, u32[]{:S(2)}) collective-permute-start(bf16[2,3,32,128]{3,2,1,0:T(8,128)(2,1)S(1)} %collective-permute-done.9.refs_6_), channel_id=1, source_target_pairs={{0,4},{2,6},{4,0},{6,2},{8,12},{10,14},{12,8},{14,10},{16,20},{18,... | collective-permute-start | bytes 147464 | tf_op jit(solution)/shard_map/ppermute | solution.py:146
  40.1 11.0 %copy-start.13 = (bf16[2,6,32,128]{3,2,1,0:T(8,128)(2,1)}, bf16[2,6,32,128]{3,2,1,0:T(8,128)(2,1)S(1)}, u32[]{:S(2)}) copy-start(bf16[2,6,32,128]{3,2,1,0:T(8,128)(2,1)S(1)} %collective-permute-done.24.refs_4_) | copy-start | bytes 294916
  40.1 11.0 %collective-permute-start.22 = (bf16[2,6,32,128]{3,2,1,0:T(8,128)(2,1)S(1)}, bf16[2,6,32,128]{3,2,1,0:T(8,128)(2,1)S(1)}, u32[]{:S(2)}, u32[]{:S(2)}) collective-permute-start(bf16[2,6,32,128]{3,2,1,0:T(8,128)(2,1)S(1)} %pad_maximum_fusion.2.refs_0_), channel_id=1, source_target_pairs={{0,8},{2,10},{4,12},{6,14},{8,0},{10,2},{12,4},{14,6},{16,24},{18,... | collective-permute-start | bytes 294920 | tf_op jit(solution)/shard_map/ppermute | solution.py:146
  40.1 13.1 %collective-permute-start.21 = (bf16[2,6,32,128]{3,2,1,0:T(8,128)(2,1)S(1)}, bf16[2,6,32,128]{3,2,1,0:T(8,128)(2,1)S(1)}, u32[]{:S(2)}, u32[]{:S(2)}) collective-permute-start(bf16[2,6,32,128]{3,2,1,0:T(8,128)(2,1)S(1)} %pad_maximum_fusion.2.refs_0_), channel_id=1, source_target_pairs={{0,4},{2,6},{4,0},{6,2},{8,12},{10,14},{12,8},{14,10},{16,20},{18,... | collective-permute-start | bytes 294920 | tf_op jit(solution)/shard_map/ppermute | solution.py:146
  41.1 12.2 %collective-permute-start.26 = (bf16[2,6,32,128]{3,2,1,0:T(8,128)(2,1)S(1)}, bf16[2,6,32,128]{3,2,1,0:T(8,128)(2,1)S(1)}, u32[]{:S(2)}, u32[]{:S(2)}) collective-permute-start(bf16[2,6,32,128]{3,2,1,0:T(8,128)(2,1)S(1)} %collective-permute-done.24.refs_4_), channel_id=1, source_target_pairs={{0,8},{2,10},{4,12},{6,14},{8,0},{10,2},{12,4},{14,6},{16,24},{18,... | collective-permute-start | bytes 294920 | tf_op jit(solution)/shard_map/ppermute | solution.py:146
  43.1 18.9 %collective-permute-start.15 = (bf16[2,3,32,512]{3,2,1,0:T(8,128)(2,1)S(1)}, bf16[2,3,32,512]{3,2,1,0:T(8,128)(2,1)S(1)}, u32[]{:S(2)}, u32[]{:S(2)}) collective-permute-start(bf16[2,3,32,512]{3,2,1,0:T(8,128)(2,1)S(1)} %get-tuple-element.21), channel_id=1, source_target_pairs={{0,2},{2,0},{4,6},{6,4},{8,10},{10,8},{12,14},{14,12},{16,18},{18,... | collective-permute-start | bytes 589832 | tf_op jit(solution)/shard_map/ppermute | solution.py:146
  47.5 21.6 %all-to-all-start.1 = ((bf16[8,2,2,16,128]{4,3,2,1,0:T(8,128)(2,1)}), bf16[8,2,2,16,128]{4,3,2,1,0:T(8,128)(2,1)S(1)}, u32[]{:S(2)}, u32[]{:S(2)}) async-start(bf16[8,2,2,16,128]{4,3,2,1,0:T(8,128)(2,1)} %y_lines.1), calls=%async_computation.1 | async-start | bytes 262144 | tf_op jit(solution)/shard_map/all_to_all | solution.py:415
  51.0 11.0 %copy-start.8 = (bf16[128,512]{1,0:T(8,128)(2,1)}, bf16[128,512]{1,0:T(8,128)(2,1)S(1)}, u32[]{:S(2)}) copy-start(bf16[128,512]{1,0:T(8,128)(2,1)S(1)} %collective-permute-done.18.m0) | copy-start | bytes 393220
  51.0 9.2 %collective-permute-start.19 = (bf16[128,512]{1,0:T(8,128)(2,1)S(1)}, bf16[128,512]{1,0:T(8,128)(2,1)S(1)}, u32[]{:S(2)}, u32[]{:S(2)}) collective-permute-start(bf16[128,512]{1,0:T(8,128)(2,1)S(1)} %collective-permute-done.17.n1), channel_id=1, source_target_pairs={{0,2},{2,0},{4,6},{6,4},{8,10},{10,8},{12,14},{14,12},{16,18},{18,... | collective-permute-start | bytes 393224 | tf_op jit(solution)/shard_map/ppermute | solution.py:146
  51.1 10.9 %copy-start.14 = (bf16[2,6,32,128]{3,2,1,0:T(8,128)(2,1)}, bf16[2,6,32,128]{3,2,1,0:T(8,128)(2,1)S(1)}, u32[]{:S(2)}) copy-start(bf16[2,6,32,128]{3,2,1,0:T(8,128)(2,1)S(1)} %collective-permute-done.22.refs_2_) | copy-start | bytes 294916
  51.2 6.8 %collective-permute-start.25 = (bf16[2,6,32,128]{3,2,1,0:T(8,128)(2,1)S(1)}, bf16[2,6,32,128]{3,2,1,0:T(8,128)(2,1)S(1)}, u32[]{:S(2)}, u32[]{:S(2)}) collective-permute-start(bf16[2,6,32,128]{3,2,1,0:T(8,128)(2,1)S(1)} %collective-permute-done.24.refs_4_), channel_id=1, source_target_pairs={{0,4},{2,6},{4,0},{6,2},{8,12},{10,14},{12,8},{14,10},{16,20},{18,... | collective-permute-start | bytes 294920 | tf_op jit(solution)/shard_map/ppermute | solution.py:146
  53.2 8.8 %copy-start.15 = (bf16[2,6,32,128]{3,2,1,0:T(8,128)(2,1)}, bf16[2,6,32,128]{3,2,1,0:T(8,128)(2,1)S(1)}, u32[]{:S(2)}) copy-start(bf16[2,6,32,128]{3,2,1,0:T(8,128)(2,1)S(1)} %collective-permute-done.21.refs_1_) | copy-start | bytes 294916
  53.2 7.0 %collective-permute-start.23 = (bf16[2,6,32,128]{3,2,1,0:T(8,128)(2,1)S(1)}, bf16[2,6,32,128]{3,2,1,0:T(8,128)(2,1)S(1)}, u32[]{:S(2)}, u32[]{:S(2)}) collective-permute-start(bf16[2,6,32,128]{3,2,1,0:T(8,128)(2,1)S(1)} %collective-permute-done.22.refs_2_), channel_id=1, source_target_pairs={{0,4},{2,6},{4,0},{6,2},{8,12},{10,14},{12,8},{14,10},{16,20},{18,... | collective-permute-start | bytes 294920 | tf_op jit(solution)/shard_map/ppermute | solution.py:146
  53.3 8.7 %copy-start.16 = (bf16[2,6,32,128]{3,2,1,0:T(8,128)(2,1)}, bf16[2,6,32,128]{3,2,1,0:T(8,128)(2,1)S(1)}, u32[]{:S(2)}) copy-start(bf16[2,6,32,128]{3,2,1,0:T(8,128)(2,1)S(1)} %collective-permute-done.26.refs_6_) | copy-start | bytes 294916
  53.3 8.7 %collective-permute-start.27 = (bf16[2,6,32,128]{3,2,1,0:T(8,128)(2,1)S(1)}, bf16[2,6,32,128]{3,2,1,0:T(8,128)(2,1)S(1)}, u32[]{:S(2)}, u32[]{:S(2)}) collective-permute-start(bf16[2,6,32,128]{3,2,1,0:T(8,128)(2,1)S(1)} %collective-permute-done.26.refs_6_), channel_id=1, source_target_pairs={{0,4},{2,6},{4,0},{6,2},{8,12},{10,14},{12,8},{14,10},{16,20},{18,... | collective-permute-start | bytes 294920 | tf_op jit(solution)/shard_map/ppermute | solution.py:146
  69.1 10.9 %copy-start.1 = (bf16[8,16,1,512]{3,1,2,0:T(8,128)(2,1)S(1)}, bf16[8,16,1,512]{3,1,2,0:T(8,128)(2,1)}, u32[]{:S(2)}) copy-start(bf16[8,16,1,512]{3,1,2,0:T(8,128)(2,1)} %param.7) | copy-start | bytes 393220
  72.3 6.0 %collective-permute-start.28 = (bf16[128,512]{1,0:T(8,128)(2,1)}, bf16[128,512]{1,0:T(8,128)(2,1)S(1)}, u32[]{:S(2)}, u32[]{:S(2)}) collective-permute-start(bf16[128,512]{1,0:T(8,128)(2,1)} %get-tuple-element.18), channel_id=1, source_target_pairs={{0,1},{1,0},{2,3},{3,2},{4,5},{5,4},{6,7},{7,6},{8,9},{9,8},{10,11... | collective-permute-start | bytes 393224 | tf_op jit(solution)/shard_map/ppermute | solution.py:150
  74.0 4.3 %collective-permute-start.29 = (bf16[128,512]{1,0:T(8,128)(2,1)}, bf16[128,512]{1,0:T(8,128)(2,1)S(1)}, u32[]{:S(2)}, u32[]{:S(2)}) collective-permute-start(bf16[128,512]{1,0:T(8,128)(2,1)} %get-tuple-element.19), channel_id=1, source_target_pairs={{0,2},{2,0},{4,6},{6,4},{8,10},{10,8},{12,14},{14,12},{16,18},{18,... | collective-permute-start | bytes 393224 | tf_op jit(solution)/shard_map/ppermute | solution.py:146
  74.0 6.0 %collective-permute-start.30 = (bf16[128,512]{1,0:T(8,128)(2,1)}, bf16[128,512]{1,0:T(8,128)(2,1)S(1)}, u32[]{:S(2)}, u32[]{:S(2)}) collective-permute-start(bf16[128,512]{1,0:T(8,128)(2,1)} %get-tuple-element.20), channel_id=1, source_target_pairs={{0,3},{1,2},{2,1},{3,0},{4,7},{5,6},{6,5},{7,4},{8,11},{9,10},{10,... | collective-permute-start | bytes 393224 | tf_op jit(solution)/shard_map/ppermute | solution.py:439
  (18 other events, 51.7 us)
